TPU v7x, 32 devices: a whole 2x2x4 slice. The times are simulated.
32 devices in a mesh: grp: 2 (over core), gx: 4 (over y, x), gy: 4 (over z).
Axes of the slice: x: 2, y: 2, z: 4, core: 2. Of those that a mesh axis runs over, the one named last changes fastest.
Arguments:
- coarse_density: float32 [512, 512, 512], P('gx', ('grp', 'gy')), may hold values from -3 to 3
- fine_density: float32 [32, 128, 256], P('gx', 'gy', 'grp'), may hold values from -96 to 96
- fine_start: float32 [32, 128, 256], P('gx', 'gy', 'grp'), may hold values from -6 to 6
- anchor: int32 [3], replicated, may hold values from 1 to 447
Outputs:
- coarse_potential: float32 [512, 512, 512], P('gx', ('grp', 'gy'))
- fine_potential: float32 [32, 128, 256], P('gx', 'gy', 'grp')
Inputs may be any that keep to these rules, and one draw needn't show every extreme that they name: Along every dimension d the coarse cells anchor[d] - 1 up to anchor[d] + (fine cells along d) / 4 lie inside the coarse grid.
All inputs are finite; a program needn't handle non-finite values.
Results may differ from a plain program's by a relative error of at most 0.00015.
Values sent between devices are 32-bit elements; how exact they have to be, the bound alone decides.
No kernel may reach another device: no remote copies, remote signals or barrier semaphores. Data moves between devices by JAX's collectives and lax.ppermute only.
A program may use at most 128 MiB of HBM per device.

v0:
```python
import math

import jax
import jax.numpy as jnp
from jax import lax
from jax.sharding import PartitionSpec as P

RATIO = 4
SWEEPS = 8


highest = lax.Precision.HIGHEST


def with_halo(block, sides, width):
    for axis, dim in sides:
        count = lax.axis_size(axis)
        forward = [(i, i + 1) for i in range(count - 1)]
        backward = [(target, source) for source, target in forward]
        low = lax.ppermute(
            lax.slice_in_dim(block, block.shape[dim] - width, None, axis=dim), axis, forward
        )
        high = lax.ppermute(lax.slice_in_dim(block, 0, width, axis=dim), axis, backward)
        block = jnp.concatenate([low, block, high], axis=dim)
    return block


def sine_table(amount):
    indices = jnp.arange(amount, dtype=jnp.int32) + 1
    product = indices[:, None] * indices[None, :] % (2 * (amount + 1))
    angles = product.astype(jnp.float32) * (math.pi / (amount + 1))
    return math.sqrt(2.0 / (amount + 1)) * jnp.sin(angles)


def eigen_values(indices, amount):
    angles = (indices + 1).astype(jnp.float32) * (math.pi / (2 * (amount + 1)))
    return -4.0 * jnp.square(jnp.sin(angles))


def interpolation(fine_index, cell_count):
    scaled = 2 * fine_index + 1 + RATIO
    bottom = scaled // (2 * RATIO)
    weight = (scaled % (2 * RATIO)).astype(jnp.float32) / (2.0 * RATIO)
    column = jnp.arange(cell_count, dtype=jnp.int32)
    first_part = jnp.where(column[None, :] == bottom[:, None], 1.0 - weight[:, None], 0.0)
    second_part = jnp.where(column[None, :] == bottom[:, None] + 1, weight[:, None], 0.0)
    return first_part + second_part


def ghost_values(face, left_matrix, right_matrix):
    partial_value = jnp.einsum("fbc,kc->fbk", face, right_matrix, precision=highest)
    return jnp.einsum("fbk,jb->fjk", partial_value, left_matrix, precision=highest)


def neighbours(padded):
    summed = padded[2:, 1:-1, 1:-1] + padded[:-2, 1:-1, 1:-1]
    summed = summed + padded[1:-1, 2:, 1:-1] + padded[1:-1, :-2, 1:-1]
    return summed + padded[1:-1, 1:-1, 2:] + padded[1:-1, 1:-1, :-2]


def selection(first_global, length, window_start, window_length):
    here = first_global + jnp.arange(length, dtype=jnp.int32)
    window = window_start + jnp.arange(window_length, dtype=jnp.int32)
    return (here[:, None] == window[None, :]).astype(jnp.float32)


def body(coarse_density, fine_density, fine_start, anchor):
    cell_count = coarse_density.shape[2]
    coarse_rows = coarse_density.shape[0]
    coarse_cols = coarse_density.shape[1]
    matrix = sine_table(cell_count)
    whole_index = jnp.arange(cell_count, dtype=jnp.int32)

    def along_first(block):
        return jnp.einsum("abc,ad->dbc", block, matrix, precision=highest)

    def along_second(block):
        return jnp.einsum("abc,bd->adc", block, matrix, precision=highest)

    def along_third(block):
        return jnp.einsum("abc,cd->abd", block, matrix, precision=highest)

    spectrum = along_third(coarse_density)
    spectrum = along_second(
        lax.all_to_all(spectrum, ("grp", "gy"), split_axis=2, concat_axis=1, tiled=True)
    )
    spectrum = along_first(lax.all_to_all(spectrum, "gx", split_axis=1, concat_axis=0, tiled=True))
    index_second = lax.axis_index("gx") * spectrum.shape[1] + jnp.arange(
        spectrum.shape[1], dtype=jnp.int32
    )
    index_third = lax.axis_index(("grp", "gy")) * spectrum.shape[2] + jnp.arange(
        spectrum.shape[2], dtype=jnp.int32
    )
    divisor = (
        eigen_values(whole_index, cell_count)[:, None, None]
        + eigen_values(index_second, cell_count)[None, :, None]
        + eigen_values(index_third, cell_count)[None, None, :]
    )
    spectrum = along_first(spectrum / divisor)
    spectrum = along_second(lax.all_to_all(spectrum, "gx", split_axis=0, concat_axis=1, tiled=True))
    potential = along_third(
        lax.all_to_all(spectrum, ("grp", "gy"), split_axis=1, concat_axis=2, tiled=True)
    )
    fine_rows, fine_cols, fine_depth = fine_start.shape
    total_x = fine_rows * lax.axis_size("gx")
    total_y = fine_cols * lax.axis_size("gy")
    total_z = fine_depth * lax.axis_size("grp")
    bound_x = total_x // RATIO + 2
    bound_y = total_y // RATIO + 2
    bound_z = total_z // RATIO + 2
    ends_x = interpolation(jnp.array([-1, total_x], dtype=jnp.int32), bound_x)
    ends_y = interpolation(jnp.array([-1, total_y], dtype=jnp.int32), bound_y)
    ends_z = interpolation(jnp.array([-1, total_z], dtype=jnp.int32), bound_z)
    coarse_x_start = lax.axis_index("gx") * coarse_rows
    coarse_y_start = lax.axis_index(("grp", "gy")) * coarse_cols
    pick_x = selection(coarse_x_start, coarse_rows, anchor[0] - 1, bound_x)
    pick_y = selection(coarse_y_start, coarse_cols, anchor[1] - 1, bound_y)
    pick_z = selection(0, cell_count, anchor[2] - 1, bound_z)
    weight_x = jnp.dot(ends_x, pick_x.T, precision=highest)
    weight_y = jnp.dot(ends_y, pick_y.T, precision=highest)
    weight_z = jnp.dot(ends_z, pick_z.T, precision=highest)
    partial_x = jnp.einsum("fx,xyz->fyz", weight_x, potential, precision=highest)
    partial_x = jnp.einsum("fyz,yb->fbz", partial_x, pick_y, precision=highest)
    partial_y = jnp.einsum("fy,xyz->fxz", weight_y, potential, precision=highest)
    partial_y = jnp.einsum("fxz,xa->faz", partial_y, pick_x, precision=highest)
    partial_z = jnp.einsum("fz,xyz->fxy", weight_z, potential, precision=highest)
    partial_z = jnp.einsum("fxy,xa->fay", partial_z, pick_x, precision=highest)
    window_x = jnp.einsum("fbz,zc->fbc", partial_x, pick_z, precision=highest)
    window_y = jnp.einsum("faz,zc->fac", partial_y, pick_z, precision=highest)
    window_z = jnp.einsum("fay,yb->fab", partial_z, pick_y, precision=highest)
    face_x, face_y, face_z = lax.psum((window_x, window_y, window_z), ("grp", "gx", "gy"))
    start_x = lax.axis_index("gx") * fine_rows
    start_y = lax.axis_index("gy") * fine_cols
    start_z = lax.axis_index("grp") * fine_depth
    values = fine_start
    index_x = start_x - 0 + jnp.arange(fine_rows + 2 * 0, dtype=jnp.int32)
    index_y = start_y - 0 + jnp.arange(fine_cols + 2 * 0, dtype=jnp.int32)
    index_z = start_z - 0 + jnp.arange(fine_depth + 2 * 0, dtype=jnp.int32)
    inner_x = interpolation(index_x, bound_x)
    inner_y = interpolation(index_y, bound_y)
    inner_z = interpolation(index_z, bound_z)
    ghost_x = ghost_values(face_x, inner_y, inner_z)
    ghost_y = ghost_values(face_y, inner_x, inner_z)
    ghost_z = ghost_values(face_z, inner_x, inner_y)
    boundary = jnp.where((index_x == 0)[:, None, None], ghost_x[0][None], 0.0)
    boundary = boundary + jnp.where((index_x == total_x - 1)[:, None, None], ghost_x[1][None], 0.0)
    boundary = boundary + jnp.where((index_y == 0)[None, :, None], ghost_y[0][:, None, :], 0.0)
    boundary = boundary + jnp.where(
        (index_y == total_y - 1)[None, :, None], ghost_y[1][:, None, :], 0.0
    )
    boundary = boundary + jnp.where((index_z == 0)[None, None, :], ghost_z[0][:, :, None], 0.0)
    boundary = boundary + jnp.where(
        (index_z == total_z - 1)[None, None, :], ghost_z[1][:, :, None], 0.0
    )
    inside_x = (index_x >= 0) & (index_x < total_x)
    inside_y = (index_y >= 0) & (index_y < total_y)
    inside_z = (index_z >= 0) & (index_z < total_z)
    inside = inside_x[:, None, None] & inside_y[None, :, None] & inside_z[None, None, :]
    boundary, inside = (boundary, inside)
    source = boundary - fine_density / (RATIO * RATIO)
    for sweep in range(SWEEPS):
        padded = with_halo(values, (("grp", 2), ("gx", 0), ("gy", 1)), 1)
        values = (neighbours(padded) + source) / 6.0
    return (potential, values)


def solution(mesh):
    return jax.shard_map(
        body,
        mesh=mesh,
        in_specs=(P("gx", ("grp", "gy"), None), P("gx", "gy", "grp"), P("gx", "gy", "grp"), P()),
        out_specs=(P("gx", ("grp", "gy"), None), P("gx", "gy", "grp")),
        check_vma=False,
    )
```

profile of v0, /device:TPU:28, one launch (start us, length us, event | category | flops | bytes accessed | tf_op | source)
XLA Modules:
  0.0 1839.5 jit_solution(12347839718840608468)
XLA Ops:
  0.6 79.9 %fusion.7 = f32[128,64,512]{0,2,1:T(8,128)S(1)} fusion(f32[128,64,512]{2,1,0:T(8,128)} %param.7, s32[512]{0:T(512)S(1)} %iota_add_fusion), kind=kOutput, calls=%fused_computation.8 | convolution fusion | flops 25772425216 | bytes 33556480 | tf_op jit(solution)/shard_map/abc,cd->abd/dot_general | solution.py:81
  80.5 18.1 copy.51
  98.6 365.7 %all_to_all.72 = f32[128,64,512]{0,1,2:T(8,128)} all-to-all(f32[128,64,512]{0,1,2:T(8,128)S(1)} %copy.51), channel_id=1, replica_groups=mesh['grp'=2,'gx'=4,'gy'=4] {'grp','gy'}, dimensions={2} | all-to-all | bytes 33554432 | tf_op jit(solution)/shard_map/all_to_all | solution.py:85
  464.3 15.2 copy.53
  479.6 68.2 %fusion.10 = f32[128,512,64]{0,1,2:T(8,128)} fusion(f32[128,512,64]{0,2,1:T(8,128)S(1)} %bitcast.135, s32[512]{0:T(512)S(1)} %iota_add_fusion), kind=kOutput, calls=%fused_computation.9 | convolution fusion | flops 25772425216 | bytes 33556480 | tf_op jit(solution)/shard_map/abc,bd->adc/dot_general | solution.py:78
  547.8 17.7 copy.56
  565.5 7.5 all-to-all-start.1
  573.3 4.0 fusion.305
  577.4 177.8 %all-to-all-done.1 = f32[128,512,64]{0,2,1:T(8,128)} async-done(((f32[128,512,64]{0,2,1:T(8,128)}), f32[128,512,64]{0,2,1:T(8,128)}, u32[]{:S(2)}, u32[]{:S(2)}) %all-to-all-start.1) | async-done | bytes 16777248 | tf_op jit(solution)/shard_map/all_to_all | solution.py:87
  755.2 17.5 copy.84
  772.7 43.7 %fusion.27 = f32[512,128,64]{1,0,2:T(8,128)S(1)} fusion(f32[512,128,64]{1,0,2:T(8,128)} %bitcast.134, s32[512]{0:T(512)S(1)} %iota_add_fusion), kind=kOutput, calls=%fused_computation.33 | convolution fusion | flops 25772425216 | bytes 33556480 | tf_op jit(solution)/shard_map/abc,ad->dbc/dot_general | solution.py:75
  816.3 30.9 %fusion.4 = f32[512,128,64]{1,0,2:T(8,128)} fusion(f32[512,128,64]{1,0,2:T(8,128)S(1)} %fusion.27, f32[64]{0:T(128)S(1)} %multiply_multiply_fusion.1, f32[512,128]{1,0:T(8,128)S(1)} %broadcast_add_fusion, f32[512,512,1]{1,0,2:T(8,128)S(1)} %fusion.305), kind=kOutput, calls=%fused_computation.5 | convolution fusion | flops 25778192384 | bytes 34865408 | tf_op jit(solution)/shard_map/abc,ad->dbc/dot_general | solution.py:75
  847.2 15.2 copy.61
  862.5 184.8 %all_to_all.73 = f32[512,128,64]{1,2,0:T(8,128)S(1)} all-to-all(f32[512,128,64]{1,2,0:T(8,128)S(1)} %copy.61), channel_id=1, replica_groups=mesh['grp'=2,'gx'=4,'gy'=4] {'gx'}, dimensions={0} | all-to-all | bytes 33554432 | tf_op jit(solution)/shard_map/all_to_all | solution.py:100
  1047.3 18.7 %copy.101 = f32[4,128,128,64]{2,0,1,3:T(4,128)} copy(f32[4,128,128,64]{2,3,1,0:T(8,128)S(1)} %bitcast.137) | data formatting | bytes 33554432 | tf_op jit(solution)/shard_map/all_to_all | solution.py:100
  1066.0 19.9 %all_to_all.63 = f32[128,512,64]{1,0,2:T(8,128)} reshape(f32[128,4,128,64]{2,1,0,3:T(4,128)} %bitcast.138) | data formatting | bytes 33554432 | tf_op jit(solution)/shard_map/all_to_all | solution.py:100
  1085.9 72.7 %convolution_bitcast_fusion = f32[128,512,64]{0,1,2:T(8,128)S(1)} fusion(f32[128,512,64]{1,0,2:T(8,128)} %all_to_all.63, s32[512]{0:T(512)S(1)} %iota_add_fusion), kind=kOutput, calls=%fused_computation.10 | convolution fusion | flops 25772425216 | bytes 33556480 | tf_op jit(solution)/shard_map/abc,bd->adc/dot_general | solution.py:78
  1158.6 21.1 %copy.64 = f32[128,512,64]{0,2,1:T(8,128)} copy(f32[128,512,64]{0,1,2:T(8,128)S(1)} %convolution_bitcast_fusion) | data formatting | bytes 33554432 | tf_op jit(solution)/shard_map/abc,bd->adc/transpose | solution.py:78
  1179.7 8.6 all-to-all-start.3
  1200.0 5.1 fusion.307
  1205.7 3.4 collective-permute-start.2
  1212.1 3.9 collective-permute-done.3
  1216.7 3.0 collective-permute-start.4
  1221.1 238.7 %all-to-all-done.3 = f32[128,512,64]{0,2,1:T(8,128)} async-done(((f32[128,512,64]{0,2,1:T(8,128)}), f32[128,512,64]{0,2,1:T(8,128)}, u32[]{:S(2)}, u32[]{:S(2)}) %all-to-all-start.3) | async-done | bytes 16777248 | tf_op jit(solution)/shard_map/all_to_all | solution.py:102
  1459.8 6.6 copy.65
  1466.4 28.4 %fusion.23 = f32[128,64,512]{2,0,1:T(8,128)S(1)} fusion(f32[128,64,512]{0,2,1:T(8,128)S(1)} %bitcast.133, f32[512,512,1]{1,0,2:T(8,128)} %fusion.307), kind=kOutput, calls=%fused_computation.32 | convolution fusion | flops 25769803776 | bytes 34603008 | tf_op jit(solution)/shard_map/abc,cd->abd/dot_general | solution.py:81
  1494.8 16.6 copy.71
  1511.4 8.3 fusion.270
  1520.4 8.5 fusion.269
  1529.6 14.4 fusion.271
  1544.4 130.8 %all-reduce = (f32[2,10,34]{2,1,0:T(8,128)S(1)}, f32[2,10,66]{2,1,0:T(8,128)S(1)}, f32[2,34,66]{2,1,0:T(8,128)S(1)}) all-reduce(f32[2,10,34]{2,1,0:T(8,128)S(1)} %fusion.152, f32[2,10,66]{2,1,0:T(8,128)S(1)} %fusion.70, f32[2,34,66]{2,1,0:T(8,128)S(1)} %fusion.72), channel_id=1, replica_groups=mesh['grp'=2,'gx'=4,'gy'=4] {'grp','gx','gy'}, use_global_device_ids=true, to_apply=%region_2.3 | all-reduce | flops 6488 | bytes 51904 | tf_op jit(solution)/shard_map/psum | solution.py:131
  1687.7 3.4 collective-permute-start.8
  1693.5 4.2 collective-permute-done.9
  1697.9 3.0 collective-permute-start.10
  1702.2 4.2 collective-permute-done.11
  1714.2 3.9 collective-permute-start.15
  1721.0 3.3 collective-permute-start.16
  1725.7 4.2 collective-permute-done.17
  1737.7 3.9 collective-permute-start.21
  1748.0 4.2 collective-permute-done.23
  1759.3 3.9 collective-permute-start.27
  1769.5 4.2 collective-permute-done.29
  1780.8 3.9 collective-permute-start.33
  1790.9 4.2 collective-permute-done.35
  1802.2 3.9 collective-permute-start.39
  1812.3 4.2 collective-permute-done.41
  1823.6 3.9 collective-permute-start.45
  1833.8 4.2 collective-permute-done.47
  (207 shorter events, 113.4 us)
Async XLA Ops:
  565.5 189.7 %all-to-all-start.1 = ((f32[128,512,64]{0,2,1:T(8,128)}), f32[128,512,64]{0,2,1:T(8,128)}, u32[]{:S(2)}, u32[]{:S(2)}) async-start(f32[128,512,64]{0,2,1:T(8,128)} %copy.56), calls=%async_computation.1 | async-start | bytes 33554432 | tf_op jit(solution)/shard_map/all_to_all | solution.py:87
  1179.7 280.1 %all-to-all-start.3 = ((f32[128,512,64]{0,2,1:T(8,128)}), f32[128,512,64]{0,2,1:T(8,128)}, u32[]{:S(2)}, u32[]{:S(2)}) async-start(f32[128,512,64]{0,2,1:T(8,128)} %copy.64), calls=%async_computation.3 | async-start | bytes 33554432 | tf_op jit(solution)/shard_map/all_to_all | solution.py:102
  1188.4 17.2 collective-permute-start
  1190.5 15.1 collective-permute-start.1
  1205.7 6.4 collective-permute-start.2
  1209.1 6.9 collective-permute-start.3
  1216.7 463.9 %collective-permute-start.4 = (f32[10,1,130]{2,1,0:T(1,128)}, f32[10,1,130]{2,1,0:T(1,128)}, u32[]{:S(2)}, u32[]{:S(2)}) collective-permute-start(f32[10,1,130]{2,1,0:T(1,128)} %get-tuple-element.27), channel_id=1, source_target_pairs={{1,0},{2,1},{3,2},{5,4},{6,5},{7,6},{9,8},{10,9},{11,10},{13,12},{... | collective-permute-start | bytes 15608 | tf_op jit(solution)/shard_map/ppermute | solution.py:23
  1219.8 460.9 %collective-permute-start.5 = (f32[10,1,130]{2,1,0:T(1,128)}, f32[10,1,130]{2,1,0:T(1,128)}, u32[]{:S(2)}, u32[]{:S(2)}) collective-permute-start(f32[10,1,130]{2,1,0:T(1,128)} %get-tuple-element.28), channel_id=1, source_target_pairs={{0,1},{1,2},{2,3},{4,5},{5,6},{6,7},{8,9},{9,10},{10,11},{12,13},{... | collective-permute-start | bytes 15608 | tf_op jit(solution)/shard_map/ppermute | solution.py:20
  1683.0 2.6 collective-permute-start.6
  1684.3 3.2 collective-permute-start.7
  1687.7 5.9 collective-permute-start.8
  1691.1 6.7 collective-permute-start.9
  1697.9 4.3 collective-permute-start.10
  1700.9 5.6 collective-permute-start.11
  1707.6 2.6 collective-permute-start.12
  1708.9 3.2 collective-permute-start.13
  1712.3 5.9 collective-permute-start.14
  1714.2 6.7 collective-permute-start.15
  1721.0 4.7 collective-permute-start.16
  1724.3 5.6 collective-permute-start.17
  1731.1 2.6 collective-permute-start.18
  1732.4 3.2 collective-permute-start.19
  1735.7 5.9 collective-permute-start.20
  1737.7 6.7 collective-permute-start.21
  1744.5 3.5 collective-permute-start.22
  1746.6 5.6 collective-permute-start.23
  1752.8 2.6 collective-permute-start.24
  1754.1 3.2 collective-permute-start.25
  1757.4 5.9 collective-permute-start.26
  1759.3 6.7 collective-permute-start.27
  1766.2 3.3 collective-permute-start.28
  1768.1 5.6 collective-permute-start.29
  1774.2 2.6 collective-permute-start.30
  1775.5 3.2 collective-permute-start.31
  1778.8 5.9 collective-permute-start.32
  1780.8 6.7 collective-permute-start.33
  1787.6 3.3 collective-permute-start.34
  1789.5 5.6 collective-permute-start.35
  1796.9 3.2 collective-permute-start.37
  1800.3 5.9 collective-permute-start.38
  1802.2 6.7 collective-permute-start.39
  1809.0 3.3 collective-permute-start.40
  1811.0 5.6 collective-permute-start.41
  1818.4 3.2 collective-permute-start.43
  1821.7 5.9 collective-permute-start.44
  1823.6 6.7 collective-permute-start.45
  1830.5 3.3 collective-permute-start.46
  1832.4 5.6 collective-permute-start.47
  (31 other events, 3341.9 us)
where the time goes:
time: 1860 us; the launch traced here: 1840 us
  blocking collectives  681 us (37%)
  waiting for transfers between devices  485 us (26%)
  matrix products  364 us (20%)
  local copies, waits for them, and re-layouts  168 us (9%)
  starting transfers between devices  114 us (6%)
  other arithmetic  23.5 us (1%)
    all_to_all x1, blocking collectives, body(): lax.all_to_all(spectrum, ('grp', 'gy'), split_axis=2, concat_axis=1, tile...  366 us
    all_to_all x1, waiting for transfers between devices, body(): lax.all_to_all(spectrum, ('grp', 'gy'), split_axis=1, concat_axis=2, tile...  239 us
    all_to_all x1, blocking collectives, body(): lax.all_to_all(spectrum, 'gx', split_axis=0, concat_axis=1, tiled=True)  185 us
    all_to_all x1, waiting for transfers between devices, body(): lax.all_to_all(spectrum, 'gx', split_axis=1, concat_axis=0, tiled=True)  178 us
    dot_general x2, matrix products, along_second(): return jnp.einsum('abc,bd->adc', block, matrix, precision=highest)  141 us
    psum x1, blocking collectives, body(): lax.psum((window_x, window_y, window_z), ('grp', 'gx', 'gy'))  131 us
    dot_general x2, matrix products, along_third(): return jnp.einsum('abc,cd->abd', block, matrix, precision=highest)  108 us
    dot_general x2, matrix products, along_first(): return jnp.einsum('abc,ad->dbc', block, matrix, precision=highest)  74.5 us
  transfers between devices with their start and end apart: 50, of which 31 were waited for; matrix products, arithmetic and copies ran while one was open for 6% of the time, Pallas kernels for 0%

commit v1 on v0

v1 whole, which is shorter than its diff:
```python
import math

import jax
import jax.numpy as jnp
from jax import lax
from jax.experimental import pallas as pl
from jax.experimental.pallas import tpu as pltpu
from jax.sharding import PartitionSpec as P

RATIO = 4
SWEEPS = 8


highest = lax.Precision.HIGHEST
high = lax.Precision.HIGH


def sine_table(amount):
    indices = jnp.arange(amount, dtype=jnp.int32) + 1
    product = indices[:, None] * indices[None, :] % (2 * (amount + 1))
    angles = product.astype(jnp.float32) * (math.pi / (amount + 1))
    return math.sqrt(2.0 / (amount + 1)) * jnp.sin(angles)


def eigen_values(indices, amount):
    angles = (indices + 1).astype(jnp.float32) * (math.pi / (2 * (amount + 1)))
    return -4.0 * jnp.square(jnp.sin(angles))


def interpolation(fine_index, cell_count):
    scaled = 2 * fine_index + 1 + RATIO
    bottom = scaled // (2 * RATIO)
    weight = (scaled % (2 * RATIO)).astype(jnp.float32) / (2.0 * RATIO)
    column = jnp.arange(cell_count, dtype=jnp.int32)
    first_part = jnp.where(column[None, :] == bottom[:, None], 1.0 - weight[:, None], 0.0)
    second_part = jnp.where(column[None, :] == bottom[:, None] + 1, weight[:, None], 0.0)
    return first_part + second_part


def ghost_values(face, left_matrix, right_matrix):
    partial_value = jnp.einsum("fbc,kc->fbk", face, right_matrix, precision=highest)
    return jnp.einsum("fbk,jb->fjk", partial_value, left_matrix, precision=highest)


def selection(first_global, length, window_start, window_length):
    here = first_global + jnp.arange(length, dtype=jnp.int32)
    window = window_start + jnp.arange(window_length, dtype=jnp.int32)
    return (here[:, None] == window[None, :]).astype(jnp.float32)


def edge_green(half_squares, length):
    theta = 2.0 * jnp.arcsinh(jnp.sqrt(half_squares))
    bottom = jnp.expm1(-2.0 * (length + 1) * theta)
    near = jnp.exp(-theta) * jnp.expm1(-2.0 * length * theta) / bottom
    far = jnp.exp(-length * theta) * jnp.expm1(-2.0 * theta) / bottom
    return near, far


def couple(first, last, near, far):
    count = len(first)
    kept, slopes, tops, scales = [last[0]], [near], [first[0]], [None]
    for p in range(1, count):
        scale = 1.0 / (1.0 - near * slopes[-1])
        top = (first[p] + near * kept[-1]) * scale
        drop = far * slopes[-1]
        kept_next = last[p] + far * kept[-1] + drop * top
        slopes_next = near + far * drop * scale
        tops.append(top)
        scales.append(scale)
        kept.append(kept_next)
        slopes.append(slopes_next)
    lows = [None] * count
    highs = [None] * count
    zero = jnp.zeros_like(first[0])
    highs[count - 1] = zero
    right = tops[count - 1]
    for p in range(count - 2, -1, -1):
        highs[p] = right
        lows[p + 1] = kept[p] + slopes[p] * right
        if p > 0:
            right = tops[p] + far * scales[p] * right
    lows[0] = zero
    return lows, highs


def with_halo(block, sides, width):
    for axis, dim, fill in sides:
        count = lax.axis_size(axis)
        forward = [(i, i + 1) for i in range(count - 1)]
        backward = [(target, source) for source, target in forward]
        low = lax.ppermute(
            lax.slice_in_dim(block, block.shape[dim] - width, None, axis=dim), axis, forward
        )
        above = lax.ppermute(lax.slice_in_dim(block, 0, width, axis=dim), axis, backward)
        parts = [block, above]
        if fill:
            shape = list(block.shape)
            shape[dim] = fill
            parts.append(jnp.zeros(shape, block.dtype))
        block = jnp.concatenate(parts + [low], axis=dim)
    return block


def halo_index(start, own, fill, width):
    own_part = start + jnp.arange(own + width, dtype=jnp.int32)
    fill_part = jnp.full((fill,), -(RATIO * RATIO * RATIO) - width, jnp.int32)
    low_part = start - width + jnp.arange(width, dtype=jnp.int32)
    return jnp.concatenate([own_part, fill_part, low_part])


def sweeps_kernel(start_ref, source_ref, inside_ref, out_ref, a_ref, b_ref):
    rows, cols, depth = start_ref.shape
    own_rows, own_cols, own_depth = out_ref.shape

    def sweep(src, dst):
        for i in range(rows):
            here = src[i]
            total = src[(i + 1) % rows] + src[(i - 1) % rows]
            total = total + pltpu.roll(here, 1, 0) + pltpu.roll(here, cols - 1, 0)
            total = total + pltpu.roll(here, 1, 1) + pltpu.roll(here, depth - 1, 1)
            dst[i] = (total + source_ref[i]) * inside_ref[i]

    a_ref[...] = start_ref[...]

    def pair(_, carry):
        sweep(a_ref, b_ref)
        sweep(b_ref, a_ref)
        return carry

    lax.fori_loop(0, SWEEPS // 2, pair, 0)
    out_ref[...] = a_ref[:own_rows, :own_cols, :own_depth]


def body(coarse_density, fine_density, fine_start, anchor):
    coarse_rows, coarse_cols, cell_count = coarse_density.shape
    count_x = lax.axis_size("gx")
    count_y = lax.axis_size("grp") * lax.axis_size("gy")
    devices = count_x * count_y
    everyone = ("gx", "grp", "gy")

    fine_rows, fine_cols, fine_depth = fine_start.shape
    total_x = fine_rows * lax.axis_size("gx")
    total_y = fine_cols * lax.axis_size("gy")
    total_z = fine_depth * lax.axis_size("grp")
    width = SWEEPS
    fill = -(fine_depth + 2 * width) % 128
    fine_pair = with_halo(
        jnp.stack([fine_start, fine_density]),
        (("grp", 3, fill), ("gx", 1, 0), ("gy", 2, 0)),
        width,
    )

    matrix_x = sine_table(coarse_rows)
    matrix_y = sine_table(coarse_cols)
    matrix_z = sine_table(cell_count)
    lam_x = eigen_values(jnp.arange(coarse_rows, dtype=jnp.int32), coarse_rows)
    lam_y = eigen_values(jnp.arange(coarse_cols, dtype=jnp.int32), coarse_cols)
    lam_z = eigen_values(jnp.arange(cell_count, dtype=jnp.int32), cell_count)
    divisor = lam_x[:, None, None] + lam_y[None, :, None] + lam_z[None, None, :]

    spectrum = jnp.einsum("abc,cd->abd", coarse_density, matrix_z, precision=high)
    spectrum = jnp.einsum("abc,bd->adc", spectrum, matrix_y, precision=high)
    spectrum = jnp.einsum("abc,ad->dbc", spectrum, matrix_x, precision=high)

    edge_x = (matrix_x[0][:, None, None], matrix_x[coarse_rows - 1][:, None, None])
    edge_y = (matrix_y[0][None, :, None], matrix_y[coarse_cols - 1][None, :, None])
    half_yz = -0.25 * (lam_y[:, None] + lam_z[None, :])
    near_x, far_x = edge_green(half_yz, coarse_rows)
    here_x = lax.axis_index("gx")

    def ghosts_x(edges):
        every = lax.all_gather(edges, "gx", axis=0)
        lows, highs = couple(
            [every[p, 0] for p in range(count_x)],
            [every[p, 1] for p in range(count_x)],
            near_x,
            far_x,
        )
        low, above = lows[0], highs[0]
        for p in range(1, count_x):
            low = jnp.where(here_x == p, lows[p], low)
            above = jnp.where(here_x == p, highs[p], above)
        return low, above

    alone = spectrum / divisor
    low_x, above_x = ghosts_x(
        jnp.stack([jnp.sum(alone * edge_x[0], axis=0), jnp.sum(alone * edge_x[1], axis=0)])
    )
    slab = (spectrum - edge_x[0] * low_x[None] - edge_x[1] * above_x[None]) / divisor
    edges = jnp.stack([jnp.sum(slab * edge_y[0], axis=1), jnp.sum(slab * edge_y[1], axis=1)])
    edges = jnp.einsum("fqk,qx->fkx", edges, matrix_x, precision=highest)
    chunk = cell_count // devices
    edges = edges.reshape(2, devices, chunk, coarse_rows).transpose(1, 0, 2, 3)
    edges = edges.reshape(devices, 2 * chunk, coarse_rows)
    edges = lax.all_to_all(edges, everyone, split_axis=0, concat_axis=0, tiled=True)
    edges = edges.reshape(count_x, count_y, 2 * chunk, coarse_rows).transpose(1, 2, 0, 3)
    edges = edges.reshape(count_y, 2 * chunk, cell_count)
    edges = jnp.einsum("pkx,xq->pkq", edges, matrix_z, precision=highest)
    mine = lax.axis_index(everyone) * chunk + jnp.arange(chunk, dtype=jnp.int32)
    half_zx = -0.25 * (eigen_values(mine, cell_count)[:, None] + lam_z[None, :])
    near_y, far_y = edge_green(half_zx, coarse_cols)
    lows, highs = couple(
        [edges[p, :chunk] for p in range(count_y)],
        [edges[p, chunk:] for p in range(count_y)],
        near_y,
        far_y,
    )
    planes = jnp.stack([jnp.concatenate(both, axis=0) for both in zip(lows, highs)])
    planes = jnp.einsum("pkq,qx->pkx", planes, matrix_z, precision=highest)
    planes = planes.reshape(count_y, 2 * chunk, count_x, coarse_rows).transpose(2, 0, 1, 3)
    planes = planes.reshape(devices, 2 * chunk, coarse_rows)
    planes = lax.all_to_all(planes, everyone, split_axis=0, concat_axis=0, tiled=True)
    planes = planes.reshape(devices, 2, chunk, coarse_rows).transpose(1, 0, 2, 3)
    planes = planes.reshape(2, cell_count, coarse_rows)
    planes = jnp.einsum("fkx,xq->fqk", planes, matrix_x, precision=highest)
    low_y, above_y = planes[0][:, None, :], planes[1][:, None, :]

    side = -(edge_y[0] * low_y + edge_y[1] * above_y)
    added = side / divisor
    more_low, more_above = ghosts_x(
        jnp.stack([jnp.sum(added * edge_x[0], axis=0), jnp.sum(added * edge_x[1], axis=0)])
    )
    low_x = (low_x + more_low)[None]
    above_x = (above_x + more_above)[None]
    spectrum = (spectrum + side - edge_x[0] * low_x - edge_x[1] * above_x) / divisor
    spectrum = jnp.einsum("abc,ad->dbc", spectrum, matrix_x, precision=high)
    spectrum = jnp.einsum("abc,bd->adc", spectrum, matrix_y, precision=high)
    potential = jnp.einsum("abc,cd->abd", spectrum, matrix_z, precision=high)

    bound_x = total_x // RATIO + 2
    bound_y = total_y // RATIO + 2
    bound_z = total_z // RATIO + 2
    coarse_x_start = lax.axis_index("gx") * coarse_rows
    coarse_y_start = lax.axis_index(("grp", "gy")) * coarse_cols
    pick_x = selection(coarse_x_start, coarse_rows, anchor[0] - 1, bound_x)
    pick_y = selection(coarse_y_start, coarse_cols, anchor[1] - 1, bound_y)
    pick_z = selection(0, cell_count, anchor[2] - 1, bound_z)

    def face(dim, total, first):
        faces = []
        for fine_index in (-1, total):
            scaled = 2 * fine_index + 1 + RATIO
            bottom = scaled // (2 * RATIO)
            weight = (scaled % (2 * RATIO)) / (2.0 * RATIO)
            value = 0.0
            for step, part in ((0, 1.0 - weight), (1, weight)):
                place = anchor[dim] - 1 + bottom + step - first
                held = (place >= 0) & (place < potential.shape[dim])
                plane = lax.dynamic_index_in_dim(
                    potential, jnp.clip(place, 0, potential.shape[dim] - 1), dim, keepdims=False
                )
                value = value + jnp.where(held, part, 0.0) * plane
            faces.append(value)
        return jnp.stack(faces)

    ends_z = interpolation(jnp.array([-1, total_z], dtype=jnp.int32), bound_z)
    weight_z = jnp.dot(ends_z, pick_z.T, precision=highest)
    partial_x = jnp.einsum("fyz,yb->fbz", face(0, total_x, coarse_x_start), pick_y, precision=highest)
    partial_y = jnp.einsum("fxz,xa->faz", face(1, total_y, coarse_y_start), pick_x, precision=highest)
    partial_z = jnp.stack([jnp.sum(potential * weight_z[f], axis=2) for f in range(2)])
    partial_z = jnp.einsum("fxy,xa->fay", partial_z, pick_x, precision=highest)
    window_x = jnp.einsum("fbz,zc->fbc", partial_x, pick_z, precision=highest)
    window_y = jnp.einsum("faz,zc->fac", partial_y, pick_z, precision=highest)
    window_z = jnp.einsum("fay,yb->fab", partial_z, pick_y, precision=highest)
    sizes = [window_x.size, window_y.size, window_z.size]
    flat = jnp.concatenate([window_x.ravel(), window_y.ravel(), window_z.ravel()])
    flat = lax.psum(flat, ("grp", "gx", "gy"))
    face_x = flat[: sizes[0]].reshape(window_x.shape)
    face_y = flat[sizes[0] : sizes[0] + sizes[1]].reshape(window_y.shape)
    face_z = flat[sizes[0] + sizes[1] :].reshape(window_z.shape)

    index_x = halo_index(lax.axis_index("gx") * fine_rows, fine_rows, 0, width)
    index_y = halo_index(lax.axis_index("gy") * fine_cols, fine_cols, 0, width)
    index_z = halo_index(lax.axis_index("grp") * fine_depth, fine_depth, fill, width)
    inner_x = interpolation(index_x, bound_x)
    inner_y = interpolation(index_y, bound_y)
    inner_z = interpolation(index_z, bound_z)
    ghost_x = ghost_values(face_x, inner_y, inner_z)
    ghost_y = ghost_values(face_y, inner_x, inner_z)
    ghost_z = ghost_values(face_z, inner_x, inner_y)
    boundary = jnp.where((index_x == 0)[:, None, None], ghost_x[0][None], 0.0)
    boundary = boundary + jnp.where((index_x == total_x - 1)[:, None, None], ghost_x[1][None], 0.0)
    boundary = boundary + jnp.where((index_y == 0)[None, :, None], ghost_y[0][:, None, :], 0.0)
    boundary = boundary + jnp.where(
        (index_y == total_y - 1)[None, :, None], ghost_y[1][:, None, :], 0.0
    )
    boundary = boundary + jnp.where((index_z == 0)[None, None, :], ghost_z[0][:, :, None], 0.0)
    boundary = boundary + jnp.where(
        (index_z == total_z - 1)[None, None, :], ghost_z[1][:, :, None], 0.0
    )
    inside_x = (index_x >= 0) & (index_x < total_x)
    inside_y = (index_y >= 0) & (index_y < total_y)
    inside_z = (index_z >= 0) & (index_z < total_z)
    inside = inside_x[:, None, None] & inside_y[None, :, None] & inside_z[None, None, :]
    source = boundary - fine_pair[1] / (RATIO * RATIO)
    shape = fine_pair.shape[1:]
    values = pl.pallas_call(
        sweeps_kernel,
        out_shape=jax.ShapeDtypeStruct(fine_start.shape, fine_start.dtype),
        scratch_shapes=[pltpu.VMEM(shape, jnp.float32), pltpu.VMEM(shape, jnp.float32)],
        name="sweeps",
    )(fine_pair[0], source, jnp.where(inside, 1.0 / 6.0, 0.0))
    return (potential, values)


def solution(mesh):
    return jax.shard_map(
        body,
        mesh=mesh,
        in_specs=(P("gx", ("grp", "gy"), None), P("gx", "gy", "grp"), P("gx", "gy", "grp"), P()),
        out_specs=(P("gx", ("grp", "gy"), None), P("gx", "gy", "grp")),
        check_vma=False,
    )
```

time: 1860 us -> 459 us (0.25)
  blocking collectives: 681 us -> 39.6 us
  waiting for transfers between devices: 485 us -> 41.6 us
  matrix products: 364 us -> 225 us
  local copies, waits for them, and re-layouts: 168 us -> 42.3 us
  starting transfers between devices: 114 us -> 25.3 us
  other arithmetic: 23.5 us -> 48.3 us
    all_to_all x2 -> x0, blocking collectives: 551 us -> none  [the longest x1 366 us: body(): lax.all_to_all(spectrum, ('grp', 'gy'), split_axis=2, concat_axis=1, tile...]
    all_to_all x2, waiting for transfers between devices: 417 us -> 14.2 us  [the longest x1 9.85 us: body(): lax.all_to_all(edges, everyone, split_axis=0, concat_axis=0, tiled=True)]
    dot_general x13 -> x12, matrix products: 356 us -> 222 us  [the longest x1 71.2 us: body(): jnp.einsum('abc,cd->abd', coarse_density, matrix_z, precision=high)]
    psum x1, blocking collectives: 131 us -> 39.6 us  [body(): flat = lax.psum(flat, ('grp', 'gx', 'gy'))]
    all_to_all x5 -> x0, local copies, waits for them, and re-layouts: 77.9 us -> none  [the longest x2 38.6 us: body(): lax.all_to_all(spectrum, 'gx', split_axis=0, concat_axis=1, tiled=True)]
    ppermute x24 -> x3, waiting for transfers between devices: 54.2 us -> 8.2 us  [with_halo(): lax.ppermute(lax.slice_in_dim(block, block.shape[dim] - width, None, axis...]
    ppermute x24 -> x3, starting transfers between devices: 49.9 us -> 6.87 us  [with_halo(): lax.ppermute(lax.slice_in_dim(block, block.shape[dim] - width, None, axis...]
    ppermute x24 -> x3, starting transfers between devices: 47.7 us -> 8.48 us  [with_halo(): lax.ppermute(lax.slice_in_dim(block, 0, width, axis=dim), axis, backward)]
  transfers between devices with their start and end apart: 50 -> 10, of which waited for: 31 -> 5; matrix products, arithmetic and copies ran while one was open for 6% -> 12% of each run, Pallas kernels for 0% -> 0%
where the time goes in v1:
time: 459 us; the launch traced here: 452 us
  matrix products  225 us (49%)
  other arithmetic  48.3 us (11%)
  local copies, waits for them, and re-layouts  42.3 us (9%)
  waiting for transfers between devices  41.6 us (9%)
  blocking collectives  39.6 us (9%)
  starting transfers between devices  25.3 us (6%)
  between operations  21.3 us (5%)
  Pallas kernels  8.53 us (2%)
    dot_general x1, matrix products, body(): jnp.einsum('abc,cd->abd', coarse_density, matrix_z, precision=high)  71.2 us
    dot_general x2, matrix products, body(): spectrum = jnp.einsum('abc,ad->dbc', spectrum, matrix_x, precision=high)  50.9 us
    dot_general x1, matrix products, body(): potential = jnp.einsum('abc,cd->abd', spectrum, matrix_z, precision=high)  45.6 us
    dot_general x2, matrix products, body(): spectrum = jnp.einsum('abc,bd->adc', spectrum, matrix_y, precision=high)  41.7 us
    psum x1, blocking collectives, body(): flat = lax.psum(flat, ('grp', 'gx', 'gy'))  39.6 us
    all_gather x2, waiting for transfers between devices, ghosts_x(): every = lax.all_gather(edges, 'gx', axis=0)  19.2 us
    unnamed x90, local copies, waits for them, and re-layouts  18.8 us
    dot_general x1, local copies, waits for them, and re-layouts, body(): jnp.einsum('abc,cd->abd', coarse_density, matrix_z, precision=high)  17.4 us
  transfers between devices with their start and end apart: 10, of which 5 were waited for; matrix products, arithmetic and copies ran while one was open for 12% of the time, Pallas kernels for 0%

profile of v1, /device:TPU:28, one launch (start us, length us, event | category | flops | bytes accessed | tf_op | source)
XLA Modules:
  0.0 451.9 jit_solution(6240979262921453878)
XLA Ops:
  7.8 71.2 %fusion.14 = f32[128,64,512]{0,2,1:T(8,128)} fusion(f32[128,64,512]{2,1,0:T(8,128)} %param.5, s32[512]{0:T(512)S(1)} %iota_add_fusion), kind=kOutput, calls=%fused_computation.27 | convolution fusion | flops 12887523328 | bytes 33556480 | tf_op jit(solution)/shard_map/abc,cd->abd/dot_general | solution.py:161
  79.0 17.4 %copy.20 = f32[128,64,512]{2,1,0:T(8,128)} copy(f32[128,64,512]{0,2,1:T(8,128)} %fusion.14) | data formatting | bytes 33554432 | tf_op jit(solution)/shard_map/abc,cd->abd/dot_general | solution.py:161
  96.4 14.7 %convolution_bitcast_fusion = f32[128,64,512]{2,1,0:T(8,128)} fusion(f32[128,64,512]{2,1,0:T(8,128)} %copy.20, s32[64]{0:T(128)S(1)} %iota_add_fusion.13), kind=kOutput, calls=%fused_computation.29 | convolution fusion | flops 1610653696 | bytes 33554688 | tf_op jit(solution)/shard_map/abc,bd->adc/dot_general | solution.py:162
  111.2 30.3 %multiply_reduce_fusion.7 = (f32[64,512]{1,0:T(8,128)S(1)}, f32[64,512]{1,0:T(8,128)S(1)}, f32[128,64,512]{2,0,1:T(8,128)}) fusion(f32[128]{0:T(128)S(1)} %get-tuple-element.72, f32[512]{0:T(512)S(1)} %multiply_multiply_fusion, f32[128,64]{0,1:T(8,128)S(1)} %broadcast_add_fusion, f32[128]{0:T(128)S(1)} %get-tuple-element.71, ...), kind=kOutput, calls=%fused_computation.26 | convolution fusion | flops 3246489600 | bytes 33852928 | tf_op jit(solution)/shard_map/abc,ad->dbc/dot_general | solution.py:163
  141.4 0.7 pad_maximum_fusion.10
  142.3 1.7 collective-permute-start
  144.0 3.1 collective-permute-start.1
  150.6 19.2 %all-gather.5.cloned.1.call-done = f32[8,64,512]{2,1,0:T(8,128)} async-done(((f32[2,64,512]{2,1,0:T(8,128)}), f32[8,64,512]{2,1,0:T(8,128)}) %all-gather.5.cloned.1.call-update) | async-done | bytes 1048592 | tf_op jit(solution)/shard_map/all_gather | solution.py:172
  169.7 1.9 select_select_fusion.1
  171.7 9.6 %multiply_reduce_fusion.5 = (f32[128,512]{1,0:T(8,128)S(1)}, f32[128,512]{1,0:T(8,128)S(1)}) fusion(f32[64]{0:T(128)S(1)} %get-tuple-element.76, f32[64]{0:T(128)S(1)} %get-tuple-element.75, f32[512]{0:T(512)S(1)} %multiply_multiply_fusion, f32[128,64]{0,1:T(8,128)S(1)} %broadcast_add_fusion, f32[64,512]{1,0:T(8,128)S(1)} %get-tuple-element.64, ...), kind=kLoop, calls=%fused_computation.24 | loop fusion | flops 41811968 | bytes 17600000 | tf_op jit(solution)/shard_map/reduce_sum | solution.py:190
  181.6 0.9 fusion.47
  182.5 0.9 copy.25
  183.3 4.9 %all-to-all-start = ((f32[32,32,128]{2,1,0:T(8,128)}), f32[32,32,128]{2,1,0:T(8,128)S(1)}, u32[]{:S(2)}, u32[]{:S(2)}) async-start(f32[32,32,128]{2,1,0:T(8,128)} %bitcast.26), calls=%async_computation | async-start | bytes 1048576 | tf_op jit(solution)/shard_map/all_to_all | solution.py:195
  191.9 9.9 %all-to-all-done = f32[32,32,128]{2,1,0:T(8,128)S(1)} async-done(((f32[32,32,128]{2,1,0:T(8,128)}), f32[32,32,128]{2,1,0:T(8,128)S(1)}, u32[]{:S(2)}, u32[]{:S(2)}) %all-to-all-start) | async-done | bytes 524320 | tf_op jit(solution)/shard_map/all_to_all | solution.py:195
  201.8 5.1 %fusion.42 = f32[8,32,512]{2,1,0:T(8,128)S(1)} fusion(f32[4,8,4,8,128]{4,3,2,1,0:T(8,128)S(1)} %bitcast.568, s32[512]{0:T(512)S(1)} %iota_add_fusion), kind=kOutput, calls=%fused_computation.64 | convolution fusion | flops 807927808 | bytes 1050624 | tf_op jit(solution)/shard_map/pkx,xq->pkq/dot_general | solution.py:198
  208.7 5.1 %convolution_bitcast_fusion.2 = f32[8,4,4,8,128]{4,3,2,1,0:T(8,128)S(1)} fusion(f32[8,32,512]{2,1,0:T(8,128)S(1)} %bitcast_dynamic-update-slice_fusion, s32[512]{0:T(512)S(1)} %iota_add_fusion), kind=kOutput, calls=%fused_computation.43 | convolution fusion | flops 807927808 | bytes 1050624 | tf_op jit(solution)/shard_map/pkq,qx->pkx/dot_general | solution.py:209
  213.8 0.9 copy.73
  214.7 4.9 %all-to-all-start.1 = ((f32[32,32,128]{2,1,0:T(8,128)}), f32[32,32,128]{2,1,0:T(8,128)S(1)}, u32[]{:S(2)}, u32[]{:S(2)}) async-start(f32[32,32,128]{2,1,0:T(8,128)} %bitcast.53), calls=%async_computation.1 | async-start | bytes 1048576 | tf_op jit(solution)/shard_map/all_to_all | solution.py:212
  220.8 0.7 broadcast_and_fusion
  221.5 0.8 fusion.79
  223.0 3.4 collective-permute-start.2
  226.4 2.5 collective-permute-start.3
  228.9 4.3 all-to-all-done.1
  233.3 1.0 convolution_bitcast_fusion.1
  234.3 8.3 %multiply_reduce_fusion.3 = (f32[64,512]{1,0:T(8,128)S(1)}, f32[64,512]{1,0:T(8,128)S(1)}) fusion(f32[128,512]{1,0:T(8,128)S(1)} %get-tuple-element.66, f32[128,512]{1,0:T(8,128)S(1)} %get-tuple-element.65, f32[64]{0:T(128)} %copy-done.11, f32[512]{0:T(512)S(1)} %multiply_multiply_fusion, f32[128,64]{0,1:T(8,128)} %copy-done.7, f32[128]{0:T(128)} %copy-done.10, ...), kind=kLoop, calls=%fused_computation.20 | loop fusion | flops 41877504 | bytes 822784 | tf_op jit(solution)/shard_map/reduce_sum | solution.py:221
  242.7 0.7 pad_maximum_fusion.11
  243.4 1.2 broadcast_compare_fusion.6
  244.6 1.4 fusion.306
  245.9 5.4 %collective-permute-done.3 = f32[2,8,32,256]{3,2,1,0:T(8,128)S(1)} collective-permute-done((f32[2,8,32,256]{3,2,1,0:T(8,128)S(1)}, f32[2,8,32,256]{3,2,1,0:T(8,128)S(1)}, u32[]{:S(2)}, u32[]{:S(2)}) %collective-permute-start.3) | collective-permute-done | bytes 524320 | tf_op jit(solution)/shard_map/ppermute | solution.py:91
  251.3 0.9 pad_maximum_fusion.8
  252.2 3.4 collective-permute-start.4
  255.7 1.3 collective-permute-start.5
  262.6 1.9 and_select_fusion.inside_ref
  264.6 0.7 copy-done.6
  265.3 2.8 collective-permute-done.5
  268.2 1.8 pad_maximum_fusion
  269.9 1.1 slice_bitcast_fusion.start_ref
  271.0 2.2 select_add_fusion.1
  273.3 1.7 select_add_fusion
  275.0 20.6 %fusion = f32[128,64,512]{2,0,1:T(8,128)} fusion(f32[128,64,512]{2,0,1:T(8,128)} %get-tuple-element.90, f32[64,512]{1,0:T(8,128)S(1)} %select_add_fusion, f32[64,512]{1,0:T(8,128)S(1)} %get-tuple-element.36, f32[128,512]{1,0:T(8,128)} %copy-done.5, f32[128,512]{1,0:T(8,128)} %copy-done.4, f32[64]{0:T(128)} %copy-done.11, f32[128]{0:T(128)} %copy-done.9, ...), kind=kOutput, calls=%fused_computation.4 | convolution fusion | flops 3267526656 | bytes 34377728 | tf_op jit(solution)/shard_map/abc,ad->dbc/dot_general | solution.py:226
  295.6 27.0 %fusion.17 = f32[128,64,512]{2,1,0:T(8,128)} fusion(f32[128,64,512]{2,0,1:T(8,128)} %fusion, s32[64]{0:T(128)S(1)} %iota_add_fusion.13), kind=kOutput, calls=%fused_computation.28 | convolution fusion | flops 1610653696 | bytes 33554688 | tf_op jit(solution)/shard_map/abc,bd->adc/dot_general | solution.py:227
  322.7 45.6 %multiply_reduce_fusion.1 = (f32[128,64]{0,1:T(8,128)S(1)}, f32[128,64]{0,1:T(8,128)S(1)}, f32[128,64,512]{2,0,1:T(8,128)}) fusion(f32[512]{0:T(512)S(1)} %bitcast.576, f32[512]{0:T(512)S(1)} %bitcast.575, s32[512]{0:T(512)S(1)} %iota_add_fusion, f32[128,64,512]{2,1,0:T(8,128)} %fusion.17), kind=kOutput, calls=%fused_computation.14 | convolution fusion | flops 12904284160 | bytes 33626112 | tf_op jit(solution)/shard_map/abc,cd->abd/dot_general | solution.py:228
  368.9 1.5 add_bitcast_fusion.1
  371.0 2.7 multiply_add_fusion.1
  374.8 39.6 %psum.7 = f32[6488]{0:T(1024)S(1)} all-reduce(f32[6488]{0:T(1024)S(1)} %concatenate.142), channel_id=1, replica_groups=mesh['grp'=2,'gx'=4,'gy'=4] {'grp','gx','gy'}, use_global_device_ids=true, to_apply=%region_8.9 | all-reduce | flops 6488 | bytes 51904 | tf_op jit(solution)/shard_map/psum | solution.py:267
  414.7 17.8 %copy.35 = f32[128,64,512]{2,1,0:T(8,128)} copy(f32[128,64,512]{2,0,1:T(8,128)} %get-tuple-element.91) | data formatting | bytes 33554432
  434.4 1.8 fusion.31.source_ref
  436.1 8.5 %sweeps.1 = f32[8,32,128]{2,1,0:T(8,128)} custom-call(f32[24,48,256]{2,1,0:T(8,128)} %slice_bitcast_fusion.start_ref, f32[24,48,256]{2,1,0:T(8,128)} %fusion.31.source_ref, f32[24,48,256]{2,1,0:T(8,128)} %and_select_fusion.inside_ref), custom_call_target="tpu_custom_call" | custom-call | tf_op jit(solution)/shard_map/sweeps/pallas_call | solution.py:297
  (181 shorter events, 15.7 us)
Async XLA Ops:
  7.2 162.6 %all-gather.5.cloned.1.call-start = ((), (), s32[]{:S(2)}) async-start(), calls=%async_computation.2 | async-start | bytes 1310720 | tf_op jit(solution)/shard_map/all_gather | solution.py:172
  7.3 162.4 %copy-start.8 = (f32[64]{0:T(128)}, f32[64]{0:T(128)S(1)}, u32[]{:S(2)}) copy-start(f32[64]{0:T(128)S(1)} %multiply_multiply_fusion.2) | copy-start | bytes 772
  7.7 163.9 %copy-start.9 = (f32[128]{0:T(128)}, f32[128]{0:T(128)S(1)}, u32[]{:S(2)}) copy-start(f32[128]{0:T(128)S(1)} %get-tuple-element.71) | copy-start | bytes 1540
  7.7 163.9 %copy-start.10 = (f32[128]{0:T(128)}, f32[128]{0:T(128)S(1)}, u32[]{:S(2)}) copy-start(f32[128]{0:T(128)S(1)} %get-tuple-element.72) | copy-start | bytes 1540
  96.4 75.2 %copy-start.7 = (f32[128,64]{0,1:T(8,128)}, f32[128,64]{0,1:T(8,128)S(1)}, u32[]{:S(2)}) copy-start(f32[128,64]{0,1:T(8,128)S(1)} %broadcast_add_fusion) | copy-start | bytes 98308
  111.1 31.0 %copy-start = (f32[8,32,128]{2,1,0:T(8,128)S(1)}, f32[8,32,128]{2,1,0:T(8,128)}, u32[]{:S(2)}) copy-start(f32[8,32,128]{2,1,0:T(8,128)} %param.6) | copy-start | bytes 393220
  111.1 31.0 %copy-start.1 = (f32[8,32,128]{2,1,0:T(8,128)S(1)}, f32[8,32,128]{2,1,0:T(8,128)}, u32[]{:S(2)}) copy-start(f32[8,32,128]{2,1,0:T(8,128)} %param.7) | copy-start | bytes 393220
  111.1 36.0 %copy-start.21 = (s32[3]{0:T(128)S(1)}, s32[3]{0:T(128)}, u32[]{:S(2)}) copy-start(s32[3]{0:T(128)} %param.8) | copy-start | bytes 40
  142.3 80.5 %collective-permute-start = (f32[2,8,32,8]{3,2,1,0:T(8,128)S(1)}, f32[2,8,32,8]{3,2,1,0:T(8,128)S(1)}, u32[]{:S(2)}, u32[]{:S(2)}) collective-permute-start(f32[2,8,32,8]{3,2,1,0:T(8,128)S(1)} %get-tuple-element.67), channel_id=1, source_target_pairs={{16,0},{17,1},{18,2},{19,3},{20,4},{21,5},{22,6},{23,7},{24,8},{25... | collective-permute-start | bytes 49160 | tf_op jit(solution)/shard_map/ppermute | solution.py:94
  144.0 78.8 %collective-permute-start.1 = (f32[2,8,32,8]{3,2,1,0:T(8,128)S(1)}, f32[2,8,32,8]{3,2,1,0:T(8,128)S(1)}, u32[]{:S(2)}, u32[]{:S(2)}) collective-permute-start(f32[2,8,32,8]{3,2,1,0:T(8,128)S(1)} %get-tuple-element.68), channel_id=1, source_target_pairs={{0,16},{1,17},{2,18},{3,19},{4,20},{5,21},{6,22},{7,23},{8,24},{9,... | collective-permute-start | bytes 49160 | tf_op jit(solution)/shard_map/ppermute | solution.py:91
  148.4 73.0 %copy-start.27 = (s32[66]{0:T(128)}, s32[66]{0:T(128)S(1)}, u32[]{:S(2)}) copy-start(s32[66]{0:T(128)S(1)} %iota_add_fusion.5) | copy-start | bytes 796
  148.6 66.1 %copy-start.22 = (s32[48]{0:T(128)}, s32[48]{0:T(128)S(1)}, u32[]{:S(2)}) copy-start(s32[48]{0:T(128)S(1)} %get-tuple-element.19) | copy-start | bytes 580
  150.5 30.7 %copy-start.11 = (f32[64]{0:T(128)}, f32[64]{0:T(128)S(1)}, u32[]{:S(2)}) copy-start(f32[64]{0:T(128)S(1)} %get-tuple-element.75) | copy-start | bytes 772
  150.6 30.7 %copy-start.12 = (f32[64]{0:T(128)}, f32[64]{0:T(128)S(1)}, u32[]{:S(2)}) copy-start(f32[64]{0:T(128)S(1)} %get-tuple-element.76) | copy-start | bytes 772
  171.6 49.8 %copy-start.41 = (f32[2]{0:T(128)S(1)}, f32[2]{0:T(128)}, u32[]{:S(2)}) copy-start(f32[2]{0:T(128)} %constant.344) | copy-start | bytes 28
  171.6 49.8 %copy-start.42 = (f32[2]{0:T(128)S(1)}, f32[2]{0:T(128)}, u32[]{:S(2)}) copy-start(f32[2]{0:T(128)} %constant.345) | copy-start | bytes 28
  171.7 49.8 %copy-start.43 = (s32[2]{0:T(128)S(1)}, s32[2]{0:T(128)}, u32[]{:S(2)}) copy-start(s32[2]{0:T(128)} %constant.346) | copy-start | bytes 28
  183.3 18.4 %all-to-all-start = ((f32[32,32,128]{2,1,0:T(8,128)}), f32[32,32,128]{2,1,0:T(8,128)S(1)}, u32[]{:S(2)}, u32[]{:S(2)}) async-start(f32[32,32,128]{2,1,0:T(8,128)} %bitcast.26), calls=%async_computation | async-start | bytes 1048576 | tf_op jit(solution)/shard_map/all_to_all | solution.py:195
  214.7 18.5 %all-to-all-start.1 = ((f32[32,32,128]{2,1,0:T(8,128)}), f32[32,32,128]{2,1,0:T(8,128)S(1)}, u32[]{:S(2)}, u32[]{:S(2)}) async-start(f32[32,32,128]{2,1,0:T(8,128)} %bitcast.53), calls=%async_computation.1 | async-start | bytes 1048576 | tf_op jit(solution)/shard_map/all_to_all | solution.py:212
  219.6 51.4 %all-gather.7.cloned.1.call-start = ((), (), s32[]{:S(2)}) async-start(), calls=%async_computation.3 | async-start | bytes 1310720 | tf_op jit(solution)/shard_map/all_gather | solution.py:172
  223.0 22.9 %collective-permute-start.2 = (f32[2,8,32,256]{3,2,1,0:T(8,128)S(1)}, f32[2,8,32,256]{3,2,1,0:T(8,128)S(1)}, u32[]{:S(2)}, u32[]{:S(2)}) collective-permute-start(f32[2,8,32,256]{3,2,1,0:T(8,128)S(1)} %pad_maximum_fusion.1), channel_id=1, source_target_pairs={{4,0},{8,4},{12,8},{5,1},{9,5},{13,9},{6,2},{10,6},{14,10},{7,3},{... | collective-permute-start | bytes 1572872 | tf_op jit(solution)/shard_map/ppermute | solution.py:94
  226.4 24.9 %collective-permute-start.3 = (f32[2,8,32,256]{3,2,1,0:T(8,128)S(1)}, f32[2,8,32,256]{3,2,1,0:T(8,128)S(1)}, u32[]{:S(2)}, u32[]{:S(2)}) collective-permute-start(f32[2,8,32,256]{3,2,1,0:T(8,128)S(1)} %pad_maximum_fusion.1), channel_id=1, source_target_pairs={{0,4},{4,8},{8,12},{1,5},{5,9},{9,13},{2,6},{6,10},{10,14},{3,7},{... | collective-permute-start | bytes 1572872 | tf_op jit(solution)/shard_map/ppermute | solution.py:91
  234.3 30.3 %copy-start.4 = (f32[128,512]{1,0:T(8,128)}, f32[128,512]{1,0:T(8,128)S(1)}, u32[]{:S(2)}) copy-start(f32[128,512]{1,0:T(8,128)S(1)} %get-tuple-element.65) | copy-start | bytes 786436
  234.3 30.2 %copy-start.5 = (f32[128,512]{1,0:T(8,128)}, f32[128,512]{1,0:T(8,128)S(1)}, u32[]{:S(2)}) copy-start(f32[128,512]{1,0:T(8,128)S(1)} %get-tuple-element.66) | copy-start | bytes 786436
  245.9 18.6 %copy-start.2 = (f32[2,8,32,256]{3,2,1,0:T(8,128)}, f32[2,8,32,256]{3,2,1,0:T(8,128)S(1)}, u32[]{:S(2)}) copy-start(f32[2,8,32,256]{3,2,1,0:T(8,128)S(1)} %collective-permute-done.2) | copy-start | bytes 1572868
  252.2 12.3 %collective-permute-start.4 = (f32[2,24,8,256]{3,2,1,0:T(8,128)}, f32[2,24,8,256]{3,2,1,0:T(8,128)S(1)}, u32[]{:S(2)}, u32[]{:S(2)}) collective-permute-start(f32[2,24,8,256]{3,2,1,0:T(8,128)} %get-tuple-element.61), channel_id=1, source_target_pairs={{1,0},{2,1},{3,2},{5,4},{6,5},{7,6},{9,8},{10,9},{11,10},{13,12},{... | collective-permute-start | bytes 1179656 | tf_op jit(solution)/shard_map/ppermute | solution.py:94
  255.7 12.5 %collective-permute-start.5 = (f32[2,24,8,256]{3,2,1,0:T(8,128)S(1)}, f32[2,24,8,256]{3,2,1,0:T(8,128)}, u32[]{:S(2)}, u32[]{:S(2)}) collective-permute-start(f32[2,24,8,256]{3,2,1,0:T(8,128)S(1)} %get-tuple-element.62), channel_id=1, source_target_pairs={{0,1},{1,2},{2,3},{4,5},{5,6},{6,7},{8,9},{9,10},{10,11},{12,13},{... | collective-permute-start | bytes 1179656 | tf_op jit(solution)/shard_map/ppermute | solution.py:91
  295.6 27.0 %copy-start.29 = (f32[1,512]{1,0:T(1,128)S(1)}, f32[1,512]{1,0:T(1,128)}, u32[]{:S(2)}) copy-start(f32[1,512]{1,0:T(1,128)} %get-tuple-element.79) | copy-start | bytes 6148
  295.6 27.0 %copy-start.30 = (f32[1,512]{1,0:T(1,128)S(1)}, f32[1,512]{1,0:T(1,128)}, u32[]{:S(2)}) copy-start(f32[1,512]{1,0:T(1,128)} %get-tuple-element.80) | copy-start | bytes 6148
  322.6 45.7 %copy-start.31 = (s32[128]{0:T(128)S(1)}, s32[128]{0:T(128)}, u32[]{:S(2)}) copy-start(s32[128]{0:T(128)} %iota_add_fusion.4) | copy-start | bytes 1540
  322.6 45.7 %copy-start.32 = (s32[10]{0:T(128)S(1)}, s32[10]{0:T(128)}, u32[]{:S(2)}) copy-start(s32[10]{0:T(128)} %iota_add_fusion.3) | copy-start | bytes 124
  322.7 45.9 %copy-start.35 = (s32[64]{0:T(128)S(1)}, s32[64]{0:T(128)}, u32[]{:S(2)}) copy-start(s32[64]{0:T(128)} %iota_add_fusion.7) | copy-start | bytes 772
  322.7 45.9 %copy-start.36 = (s32[34]{0:T(128)S(1)}, s32[34]{0:T(128)}, u32[]{:S(2)}) copy-start(s32[34]{0:T(128)} %iota_add_fusion.6) | copy-start | bytes 412
  322.7 48.0 %copy-start.28 = (s32[66]{0:T(128)S(1)}, s32[66]{0:T(128)}, u32[]{:S(2)}) copy-start(s32[66]{0:T(128)} %copy-done.27) | copy-start | bytes 796
  414.5 18.3 %copy-start.15 = (f32[48]{0:T(128)S(1)}, f32[48]{0:T(128)}, u32[]{:S(2)}) copy-start(f32[48]{0:T(128)} %get-tuple-element.31) | copy-start | bytes 580
  414.5 18.3 %copy-start.16 = (f32[48]{0:T(128)S(1)}, f32[48]{0:T(128)}, u32[]{:S(2)}) copy-start(f32[48]{0:T(128)} %get-tuple-element.32) | copy-start | bytes 580
  414.6 18.3 %copy-start.19 = (s32[48]{0:T(128)S(1)}, s32[48]{0:T(128)}, u32[]{:S(2)}) copy-start(s32[48]{0:T(128)} %get-tuple-element.34) | copy-start | bytes 580
  414.6 18.3 %copy-start.20 = (s32[48]{0:T(128)S(1)}, s32[48]{0:T(128)}, u32[]{:S(2)}) copy-start(s32[48]{0:T(128)} %get-tuple-element.35) | copy-start | bytes 580
  414.6 18.9 %copy-start.13 = (f32[24]{0:T(128)S(1)}, f32[24]{0:T(128)}, u32[]{:S(2)}) copy-start(f32[24]{0:T(128)} %get-tuple-element.26) | copy-start | bytes 292
  414.6 18.9 %copy-start.14 = (f32[24]{0:T(128)S(1)}, f32[24]{0:T(128)}, u32[]{:S(2)}) copy-start(f32[24]{0:T(128)} %get-tuple-element.27) | copy-start | bytes 292
  414.6 18.9 %copy-start.17 = (s32[24]{0:T(128)S(1)}, s32[24]{0:T(128)}, u32[]{:S(2)}) copy-start(s32[24]{0:T(128)} %get-tuple-element.29) | copy-start | bytes 292
  414.6 18.9 %copy-start.18 = (s32[24]{0:T(128)S(1)}, s32[24]{0:T(128)}, u32[]{:S(2)}) copy-start(s32[24]{0:T(128)} %get-tuple-element.30) | copy-start | bytes 292
  414.6 19.7 %copy-start.33 = (pred[256]{0:T(512)(128)(4,1)S(1)}, pred[256]{0:T(512)(128)(4,1)}, u32[]{:S(2)}) copy-start(pred[256]{0:T(512)(128)(4,1)} %get-tuple-element.81) | copy-start | bytes 772
  414.6 19.7 %copy-start.34 = (pred[256]{0:T(512)(128)(4,1)S(1)}, pred[256]{0:T(512)(128)(4,1)}, u32[]{:S(2)}) copy-start(pred[256]{0:T(512)(128)(4,1)} %get-tuple-element.82) | copy-start | bytes 772
  414.6 19.7 %copy-start.37 = (pred[24]{0:T(512)(128)(4,1)S(1)}, pred[24]{0:T(512)(128)(4,1)}, u32[]{:S(2)}) copy-start(pred[24]{0:T(512)(128)(4,1)} %get-tuple-element.83) | copy-start | bytes 76
  414.6 19.7 %copy-start.38 = (pred[24]{0:T(512)(128)(4,1)S(1)}, pred[24]{0:T(512)(128)(4,1)}, u32[]{:S(2)}) copy-start(pred[24]{0:T(512)(128)(4,1)} %get-tuple-element.84) | copy-start | bytes 76
  414.7 19.7 %copy-start.39 = (pred[48]{0:T(512)(128)(4,1)S(1)}, pred[48]{0:T(512)(128)(4,1)}, u32[]{:S(2)}) copy-start(pred[48]{0:T(512)(128)(4,1)} %get-tuple-element.85) | copy-start | bytes 148
  414.7 19.7 %copy-start.40 = (pred[48]{0:T(512)(128)(4,1)S(1)}, pred[48]{0:T(512)(128)(4,1)}, u32[]{:S(2)}) copy-start(pred[48]{0:T(512)(128)(4,1)} %get-tuple-element.86) | copy-start | bytes 148
  (6 other events, 86.4 us)
Sparse Core Ops, SparseCore 0:
  142.3 27.4 all-gather.4
  243.5 26.6 all-gather.6
